TPU v7x, 128 devices: a whole 4x4x4 slice. The times are simulated.
128 devices in a mesh: dp: 16 (over z, y), mp: 8 (over x, core).
Axes of the slice: x: 4, y: 4, z: 4, core: 2. Of those that a mesh axis runs over, the one named last changes fastest.
Arguments:
- tokens: bfloat16 [32768, 1536], P(('dp', 'mp')), may hold values from -6 to 6
- lengths: int32 [16, 4], P('dp'), may hold values from 1 to 1024, 2048 in all within a row
- request_adapter: int32 [16, 4], P('dp'), may hold values from 0 to 15
- group_page_slots: int32 [16, 16], P('dp'), may hold values from 0 to 15, as said below
- routes: int32 [32768, 4], P(('dp', 'mp')), may hold values from 0 to 31, all different within a row; in each aligned block of 256 rows (0 to 255, 256 to 511, ...) at most 48 rows name the same one
- attention_gain: float32 [1536], replicated, may hold values from 0.1 to 1.9
- query_key_value_weight: bfloat16 [1536, 2048], P(None, 'mp')
- adapter_down_weight: bfloat16 [16, 1536, 16], P('dp'), may hold values from -0.15625 to 0.15625
- adapter_up_weight: bfloat16 [16, 16, 1536], P('dp'), may hold values from -0.75 to 0.75
- output_weight: bfloat16 [1536, 1536], P(None, 'mp'), may hold values from -0.15625 to 0.15625
- expert_norm_gain: float32 [1536], replicated, may hold values from 0.1 to 1.9
- router: bfloat16 [1536, 32], replicated, may hold values from -0.3125 to 0.3125
- expert_gate_up_weight: bfloat16 [32, 1536, 1536], P('dp'), may hold values from -0.15625 to 0.15625
- expert_down_weight: bfloat16 [32, 768, 1536], P('dp'), may hold values from -0.21875 to 0.21875
Outputs:
- layer_out: bfloat16 [32768, 1536], P(('dp', 'mp'))
- kv_pool: bfloat16 [256, 128, 512], P(('dp', 'mp'))
Inputs may be any that keep to these rules, and one draw needn't show every extreme that they name: `lengths`: each row sums to 2048, and its longest length is exactly half of 2048. `group_page_slots`: each row is a permutation of the 16 slots of its group. `routes`: A token names 4 different experts; among the rows of one device no expert is named more than 48 times.
All inputs are finite; a program needn't handle non-finite values.
Results may differ from a plain program's by a relative error of at most 0.02.
The roundings to bfloat16 on the way count: a program that leaves them out, or rounds other values in their place, can miss the bound.
Values may be sent and summed in bfloat16 or wider, within the bound.
A program may use at most 128 MiB of HBM per device.

v0:
```python
import jax
import jax.numpy as jnp
from jax import lax
from jax.sharding import PartitionSpec as P

HEAD_SIZE = 128
PAGE = 128
CAP = 48
eps = 1e-06
neg_fill = -1e30


def rms_norm(values, gains):
    widened = values.astype(jnp.float32)
    inv_rms = lax.rsqrt(jnp.mean(widened * widened, axis=-1, keepdims=True) + eps)
    return (widened * inv_rms * gains).astype(jnp.bfloat16)


def segment_ids(length_row, offset, count):
    seq_ends = jnp.cumsum(length_row)
    positions = offset + jnp.arange(count, dtype=jnp.int32)
    return jnp.sum((positions[:, None] >= seq_ends[None, :]).astype(jnp.int32), axis=1)


def shards(
    tokens,
    lengths,
    request_adapter,
    group_page_slots,
    routes,
    attention_gain,
    query_key_value_weight,
    adapter_down_weight,
    adapter_up_weight,
    output_weight,
    expert_norm_gain,
    router,
    expert_gate_up_weight,
    expert_down_weight,
):
    adapter_down_map, adapter_up_map = (
        lax.all_gather(adapter_down_weight, "dp", axis=0, tiled=True),
        lax.all_gather(adapter_up_weight, "dp", axis=0, tiled=True),
    )
    tokens_per_shard = tokens.shape[0]
    model_columns = tokens.shape[1]
    mp_index = lax.axis_index("mp")
    group_start = mp_index * tokens_per_shard
    length_row = lengths[0]
    query_seg = segment_ids(length_row, group_start, tokens_per_shard)
    normalized_input = rms_norm(tokens, attention_gain)
    full_qkv, full_out = (
        lax.all_gather(query_key_value_weight, "mp", axis=1, tiled=True),
        lax.all_gather(output_weight, "mp", axis=1, tiled=True),
    )
    complete_query_key_value = jnp.dot(
        normalized_input, full_qkv, preferred_element_type=jnp.float32
    )
    seq_count = lengths.shape[1]
    seq_match = (query_seg[:, None] == jnp.arange(seq_count, dtype=jnp.int32)[None, :]).astype(
        jnp.int32
    )
    token_adapter = jnp.sum(seq_match * request_adapter[0][None, :], axis=1)
    adapter_total = adapter_down_map.shape[0]
    adapter_rank_size = adapter_down_map.shape[2]
    query_width = adapter_up_map.shape[2]
    flattened_down = jnp.transpose(adapter_down_map, (1, 0, 2)).reshape(
        model_columns, adapter_total * adapter_rank_size
    )
    adapter_middle = jnp.dot(
        normalized_input, flattened_down, preferred_element_type=jnp.float32
    ).reshape(tokens_per_shard, adapter_total, adapter_rank_size)
    adapter_selected = token_adapter[:, None] == jnp.arange(adapter_total, dtype=jnp.int32)[None, :]
    adapter_middle = (
        jnp.where(adapter_selected[:, :, None], adapter_middle, 0.0)
        .astype(jnp.bfloat16)
        .reshape(tokens_per_shard, adapter_total * adapter_rank_size)
    )
    adapter_query = jnp.dot(
        adapter_middle,
        adapter_up_map.reshape(adapter_total * adapter_rank_size, query_width),
        preferred_element_type=jnp.float32,
    )
    query_rows = (complete_query_key_value[:, :query_width] + adapter_query).astype(jnp.bfloat16)
    key_value = complete_query_key_value[:, query_width:].astype(jnp.bfloat16)
    kv_dim = key_value.shape[1] // 2
    group_kv = lax.all_gather(key_value, "mp", axis=0, tiled=True)
    group_len = group_kv.shape[0]
    key_seg = segment_ids(length_row, 0, group_len)
    key_pos = jnp.arange(group_len, dtype=jnp.int32)
    query_pos = group_start + jnp.arange(tokens_per_shard, dtype=jnp.int32)
    allowed = (query_seg[:, None] == key_seg[None, :]) & (key_pos[None, :] <= query_pos[:, None])
    n_kv = kv_dim // HEAD_SIZE
    group_share = query_width // kv_dim
    pieces = []
    for head_position in range(n_kv):
        lo_col = head_position * group_share * HEAD_SIZE
        q_head = query_rows[:, lo_col : lo_col + group_share * HEAD_SIZE].reshape(
            tokens_per_shard, group_share, HEAD_SIZE
        )
        k_head = group_kv[:, head_position * HEAD_SIZE : (head_position + 1) * HEAD_SIZE]
        v_head = group_kv[
            :, kv_dim + head_position * HEAD_SIZE : kv_dim + (head_position + 1) * HEAD_SIZE
        ]
        scores = jnp.einsum(
            "tgd,sd->tgs", q_head, k_head, preferred_element_type=jnp.float32
        ) * HEAD_SIZE ** (-0.5)
        scores = jnp.where(allowed[:, None, :], scores, neg_fill)
        row_max = jnp.max(scores, axis=2, keepdims=True)
        expd = jnp.exp(scores - row_max)
        probs = (expd / jnp.sum(expd, axis=2, keepdims=True)).astype(jnp.bfloat16)
        mixed = jnp.einsum("tgs,sd->tgd", probs, v_head, preferred_element_type=jnp.float32)
        pieces.append(mixed.astype(jnp.bfloat16).reshape(tokens_per_shard, group_share * HEAD_SIZE))
    attended = jnp.concatenate(pieces, axis=1)
    projected = jnp.dot(attended, full_out, preferred_element_type=jnp.float32)
    residual = (tokens.astype(jnp.float32) + projected).astype(jnp.bfloat16)
    pages_dev = tokens_per_shard // PAGE
    pages_grp = group_page_slots.shape[1]
    my_slots = mp_index * pages_dev + jnp.arange(pages_dev, dtype=jnp.int32)
    slot_match = (group_page_slots[0][None, :] == my_slots[:, None]).astype(jnp.int32)
    source_page = jnp.sum(slot_match * jnp.arange(pages_grp, dtype=jnp.int32)[None, :], axis=1)
    pool = group_kv.reshape(pages_grp, PAGE, 2 * kv_dim)[source_page]
    ffn_in = rms_norm(residual, expert_norm_gain)
    logits = jnp.dot(ffn_in, router, preferred_element_type=jnp.float32)
    chosen = jnp.take_along_axis(logits, routes, axis=1)
    route_weights = jax.nn.softmax(chosen, axis=1)
    n_exp = router.shape[1]
    top_k = routes.shape[1]
    pair_expert = routes.reshape(-1)
    expert_hits = (pair_expert[:, None] == jnp.arange(n_exp, dtype=jnp.int32)[None, :]).astype(
        jnp.int32
    )
    slot_index = jnp.sum((jnp.cumsum(expert_hits, axis=0) - 1) * expert_hits, axis=1)
    target = pair_expert * CAP + slot_index
    send_rows = (
        jnp.zeros((n_exp * CAP, model_columns), jnp.bfloat16)
        .at[target]
        .set(jnp.repeat(ffn_in, top_k, axis=0))
    )
    n_dp = lax.axis_size("dp")
    exp_local = n_exp // n_dp
    outgoing = send_rows.reshape(n_dp, exp_local, CAP, model_columns)
    arrived = lax.all_to_all(outgoing, "dp", split_axis=0, concat_axis=0, tiled=True)
    gate_up = jnp.einsum(
        "secd,edf->secf", arrived, expert_gate_up_weight, preferred_element_type=jnp.float32
    )
    hidden_units = expert_down_weight.shape[1]
    active = (jnp.maximum(gate_up[..., :hidden_units], 0.0) * gate_up[..., hidden_units:]).astype(
        jnp.bfloat16
    )
    produced = jnp.einsum(
        "secf,efd->secd", active, expert_down_weight, preferred_element_type=jnp.float32
    ).astype(jnp.bfloat16)
    returned = lax.all_to_all(produced, "dp", split_axis=0, concat_axis=0, tiled=True)
    pair_out = (
        returned.reshape(n_exp * CAP, model_columns)[target]
        .astype(jnp.float32)
        .reshape(tokens_per_shard, top_k, model_columns)
    )
    mixture = jnp.sum(pair_out * route_weights[:, :, None], axis=1)
    layer_out = (residual.astype(jnp.float32) + mixture).astype(jnp.bfloat16)
    return (layer_out, pool)


def solution(mesh):
    return jax.shard_map(
        shards,
        mesh=mesh,
        in_specs=(
            P(("dp", "mp"), None),
            P("dp", None),
            P("dp", None),
            P("dp", None),
            P(("dp", "mp"), None),
            P(),
            P(None, "mp"),
            P("dp", None, None),
            P("dp", None, None),
            P(None, "mp"),
            P(),
            P(),
            P("dp", None, None),
            P("dp", None, None),
        ),
        out_specs=(P(("dp", "mp"), None), P(("dp", "mp"), None, None)),
        check_vma=False,
    )
```

profile of v0, /device:TPU:6, one launch (start us, length us, event | category | flops | bytes accessed | tf_op | source)
XLA Modules:
  0.0 358.5 jit_solution(10791619385420463547)
XLA Ops:
  8.0 1.4 fusion.32
  9.4 46.9 %all-gather.4.cloned.1.call-done = bf16[1536,2048]{1,0:T(8,128)(2,1)} async-done(((bf16[1536,256]{1,0:T(8,128)(2,1)}), bf16[1536,2048]{1,0:T(8,128)(2,1)}) %all-gather.4.cloned.1.call-update) | async-done | bytes 6291472 | tf_op jit(solution)/shard_map/all_gather | solution.py:53
  56.3 4.9 %fusion.49 = f32[256,2048]{1,0:T(8,128)S(1)} fusion(bf16[1536,2048]{1,0:T(8,128)(2,1)} %all-gather.4.cloned.1.call-done, bf16[256,1536]{1,0:T(8,128)(2,1)} %param.14, f32[1536]{0:T(1024)} %param.19, f32[256]{0:T(256)S(1)} %add_rsqrt_fusion.1), kind=kOutput, calls=%fused_computation.68 | convolution fusion | flops 1612185600 | bytes 9182208 | tf_op jit(solution)/shard_map/dot_general | solution.py:56
  61.2 1.3 copy-done.11
  65.0 25.1 %all_gather.16 = bf16[16,1536,16]{1,2,0:T(8,128)(2,1)S(1)} all-gather(bf16[1,1536,16]{1,2,0:T(8,128)(2,1)S(1)} %copy-done.9), channel_id=1, replica_groups=mesh['dp'=16,'mp'=8] {'dp'}, dimensions={0}, use_global_device_ids=true | all-gather | bytes 835584 | tf_op jit(solution)/shard_map/all_gather | solution.py:42
  90.1 9.0 %reduce-window.19 = s32[32,8,128]{2,1,0:T(8,128)S(1)} reduce-window(s32[32,8,128]{2,1,0:T(8,128)S(1)} %fusion.54, s32[]{:T(128)} %constant.20.clone.1), window={size=1x1x128 pad=0_0x0_0x127_0}, to_apply=%region_9.10 | reduce-window | flops 4161536 | bytes 262148 | tf_op jit(solution)/shard_map/reduce-window.1
  99.9 23.2 %all_gather.17 = bf16[16,16,1536]{2,1,0:T(8,128)(2,1)S(1)} all-gather(bf16[1,16,1536]{2,1,0:T(8,128)(2,1)S(1)} %copy-done.10), channel_id=1, replica_groups=mesh['dp'=16,'mp'=8] {'dp'}, dimensions={0}, use_global_device_ids=true | all-gather | bytes 835584 | tf_op jit(solution)/shard_map/all_gather | solution.py:43
  123.8 1.5 fusion.31
  125.3 2.6 fusion.26
  128.4 7.3 %fusion.46 = f32[256,6,2048]{2,0,1:T(8,128)} fusion(bf16[256,6,128]{0,2,1:T(8,128)(2,1)S(1)} %bitcast.93, bf16[2048,512]{1,0:T(8,128)(2,1)} %all-gather.6.cloned.1.call-done), kind=kOutput, calls=%fused_computation.66 | convolution fusion | flops 805306368 | bytes 13500416 | tf_op jit(solution)/shard_map/tgd,sd->tgs/dot_general | solution.py:105
  135.7 2.9 fusion.45
  138.6 17.6 %fusion.70 = (f32[256,6]{0,1:T(8,128)S(1)}, f32[256,6,2048]{2,0,1:T(8,128)}) fusion(f32[256,6,2048]{2,0,1:T(8,128)} %fusion.46, pred[256,2048]{1,0:T(8,128)(4,1)} %fusion.31), kind=kOutput, calls=%fused_computation.112 | output fusion | flops 18876416 | bytes 25696256 | tf_op jit(solution)/shard_map/sub | solution.py:110
  156.2 9.5 %fusion.69 = (f32[256,6]{0,1:T(8,128)S(1)}, f32[256,6,2048]{2,0,1:T(8,128)}) fusion(f32[256,6,2048]{2,0,1:T(8,128)S(1)} %fusion.45, pred[256,2048]{1,0:T(8,128)(4,1)} %fusion.31), kind=kOutput, calls=%fused_computation.111 | output fusion | flops 18876416 | bytes 25696256 | tf_op jit(solution)/shard_map/sub | solution.py:110
  165.7 7.0 %fusion.36 = bf16[256,6,128]{0,2,1:T(8,128)(2,1)S(1)} fusion(f32[256,6,2048]{2,0,1:T(8,128)} %get-tuple-element.9, f32[256,6]{0,1:T(8,128)S(1)} %get-tuple-element.8, bf16[2048,512]{1,0:T(8,128)(2,1)} %all-gather.6.cloned.1.call-done), kind=kOutput, calls=%fused_computation.53 | convolution fusion | flops 811794432 | bytes 13506560 | tf_op jit(solution)/shard_map/tgs,sd->tgd/dot_general | solution.py:112
  172.7 1.3 copy-done.18
  174.0 3.7 %fusion.35 = bf16[256,6,128]{0,2,1:T(8,128)(2,1)S(1)} fusion(f32[256,6,2048]{2,0,1:T(8,128)S(1)} %copy-done.18, f32[256,6]{0,1:T(8,128)S(1)} %get-tuple-element.6, bf16[2048,512]{1,0:T(8,128)(2,1)} %all-gather.6.cloned.1.call-done), kind=kOutput, calls=%fused_computation.52 | convolution fusion | flops 811794432 | bytes 13506560 | tf_op jit(solution)/shard_map/tgs,sd->tgd/dot_general | solution.py:112
  177.7 3.9 %multiply_reduce_fusion.1 = (f32[256]{0:T(256)S(1)}, f32[256,1536]{1,0:T(8,128)S(1)}) fusion(bf16[1536,1536]{0,1:T(8,128)(2,1)} %all-gather.8.cloned.1.call-done, bf16[256,768]{0,1:T(8,128)(2,1)S(1)} %bitcast.107, bf16[256,768]{0,1:T(8,128)(2,1)S(1)} %bitcast.106, bf16[256,1536]{1,0:T(8,128)(2,1)S(1)} %copy-done.6), kind=kOutput, calls=%fused_computation.51 | convolution fusion | flops 1211891456 | bytes 7865344 | tf_op jit(solution)/shard_map/dot_general | solution.py:115
  181.6 1.2 copy-done.3
  184.7 2.6 reshape.285
  187.3 9.2 %scatter_custom_fusion = bf16[1536,1536]{1,0:T(8,128)(2,1)} fusion(s32[1024]{0:T(1024)S(1)} %bitcast.99, bf16[1024,1536]{1,0:T(8,128)(2,1)} %reshape.285, bf16[]{:T(256)} %constant.34.clone.1), kind=kCustom, calls=%fused_computation.42 | custom fusion | bytes 4719104 | tf_op jit(solution)/shard_map/scatter | solution.py:138
  196.5 54.8 %all_to_all.10 = bf16[16,2,48,1536]{3,2,1,0:T(8,128)(2,1)S(1)} all-to-all(bf16[16,2,48,1536]{3,2,1,0:T(8,128)(2,1)} %bitcast.92), channel_id=1, replica_groups=mesh['dp'=16,'mp'=8] {'dp'}, dimensions={0} | all-to-all | bytes 9437184 | tf_op jit(solution)/shard_map/all_to_all | solution.py:143
  251.3 10.0 %fusion.14 = f32[16,2,48,1536]{3,2,0,1:T(8,128)S(1)} fusion(bf16[2,1536,1536]{2,1,0:T(8,128)(2,1)} %param.26, bf16[16,2,48,1536]{3,2,1,0:T(8,128)(2,1)S(1)} %all_to_all.10), kind=kOutput, calls=%fused_computation.25 | convolution fusion | flops 7247757312 | bytes 23592960 | tf_op jit(solution)/shard_map/secd,edf->secf/dot_general | solution.py:144
  261.2 6.4 %convert_bitcast_fusion = bf16[16,2,48,1536]{3,2,0,1:T(8,128)(2,1)S(1)} fusion(bf16[2,768,1536]{2,1,0:T(8,128)(2,1)} %param.27, f32[16,2,48,1536]{3,2,0,1:T(8,128)S(1)} %fusion.14), kind=kOutput, calls=%fused_computation.32 | convolution fusion | flops 3629776896 | bytes 18874368 | tf_op jit(solution)/shard_map/secf,efd->secd/dot_general | solution.py:151
  267.6 2.6 copy.87
  270.2 4.9 %all-to-all-start.1 = ((bf16[16,2,48,1536]{3,2,1,0:T(8,128)(2,1)}), bf16[16,2,48,1536]{3,2,1,0:T(8,128)(2,1)}, u32[]{:S(2)}, u32[]{:S(2)}) async-start(bf16[16,2,48,1536]{3,2,1,0:T(8,128)(2,1)} %copy.87), calls=%async_computation.1 | async-start | bytes 9437184 | tf_op jit(solution)/shard_map/all_to_all | solution.py:154
  276.0 8.7 %gather_fusion.2 = f32[1024]{0:T(1024)S(1)} fusion(f32[256,32]{0,1:T(8,128)S(1)} %fusion.71, s32[1024]{0:T(1024)S(1)} %reshape.275), kind=kCustom, calls=%fused_computation.2 | custom fusion | bytes 16384 | tf_op jit(solution)/shard_map/jit(take_along_axis)/gather | solution.py:125
  285.1 2.9 gather_fusion.1
  288.0 41.7 %all-to-all-done.1 = bf16[16,2,48,1536]{3,2,1,0:T(8,128)(2,1)} async-done(((bf16[16,2,48,1536]{3,2,1,0:T(8,128)(2,1)}), bf16[16,2,48,1536]{3,2,1,0:T(8,128)(2,1)}, u32[]{:S(2)}, u32[]{:S(2)}) %all-to-all-start.1) | async-done | bytes 4718624 | tf_op jit(solution)/shard_map/all_to_all | solution.py:154
  329.7 9.6 %gather_fusion = bf16[1024,1536]{1,0:T(8,128)(2,1)S(1)} fusion(bf16[1536,1536]{1,0:T(8,128)(2,1)} %bitcast.28, s32[1024]{0:T(1024)S(1)} %broadcast_clamp_fusion), kind=kCustom, calls=%fused_computation | custom fusion | bytes 6295552 | tf_op jit(solution)/shard_map/gather | solution.py:156
  339.3 3.9 %reshape.258 = f32[256,4,1536]{2,1,0:T(4,128)} reshape(bf16[1024,1536]{1,0:T(8,128)(2,1)S(1)} %gather_fusion) | data formatting | bytes 9437184 | tf_op jit(solution)/shard_map/convert_element_type | solution.py:157
  343.1 7.5 %multiply_reduce_fusion = f32[256,1536]{1,0:T(8,128)S(1)} fusion(f32[256,4,1536]{2,1,0:T(4,128)} %reshape.258, f32[256,4]{1,0:T(8,128)S(1)} %copy.90), kind=kLoop, calls=%fused_computation.16 | loop fusion | flops 2752512 | bytes 7868416 | tf_op jit(solution)/shard_map/reduce_sum | solution.py:160
  350.7 1.1 add_convert_fusion
  (87 shorter events, 8.0 us)
Async XLA Ops:
  7.2 268.5 %copy-start = (bf16[1536,32]{0,1:T(8,128)(2,1)S(1)}, bf16[1536,32]{0,1:T(8,128)(2,1)}, u32[]{:S(2)}) copy-start(bf16[1536,32]{0,1:T(8,128)(2,1)} %param.25) | copy-start | bytes 294916
  7.2 49.2 %all-gather.4.cloned.1.call-start = ((), (), s32[]{:S(2)}) async-start(), calls=%async_computation.2 | async-start | bytes 7077888 | tf_op jit(solution)/shard_map/all_gather | solution.py:53
  7.9 120.4 %all-gather.6.cloned.1.call-start = ((), (), s32[]{:S(2)}) async-start(), calls=%async_computation.3 | async-start | bytes 2359296 | tf_op jit(solution)/shard_map/all_gather | solution.py:87
  9.3 54.8 %copy-start.7 = (s32[256,4]{0,1:T(4,128)S(1)}, s32[256,4]{0,1:T(4,128)}, u32[]{:S(2)}) copy-start(s32[256,4]{0,1:T(4,128)} %param.18) | copy-start | bytes 12292
  9.3 55.2 %copy-start.16 = (s32[1,4]{1,0:T(1,128)S(1)}, s32[1,4]{1,0:T(1,128)}, u32[]{:S(2)}) copy-start(s32[1,4]{1,0:T(1,128)} %param.15) | copy-start | bytes 52
  9.4 55.5 %copy-start.14 = (s32[1,4]{1,0:T(1,128)S(1)}, s32[1,4]{1,0:T(1,128)}, u32[]{:S(2)}) copy-start(s32[1,4]{1,0:T(1,128)} %param.16) | copy-start | bytes 52
  9.4 55.6 %copy-start.9 = (bf16[1,1536,16]{1,2,0:T(8,128)(2,1)S(1)}, bf16[1,1536,16]{1,2,0:T(8,128)(2,1)}, u32[]{:S(2)}) copy-start(bf16[1,1536,16]{1,2,0:T(8,128)(2,1)} %param.21) | copy-start | bytes 147460
  9.4 90.5 %copy-start.10 = (bf16[1,16,1536]{2,1,0:T(8,128)(2,1)S(1)}, bf16[1,16,1536]{2,1,0:T(8,128)(2,1)}, u32[]{:S(2)}) copy-start(bf16[1,16,1536]{2,1,0:T(8,128)(2,1)} %param.22) | copy-start | bytes 147460
  61.2 1.4 copy-start.11
  62.6 62.7 %copy-start.5 = (bf16[256,1536]{1,0:T(8,128)(2,1)S(1)}, bf16[256,1536]{1,0:T(8,128)(2,1)}, u32[]{:S(2)}) copy-start(bf16[256,1536]{1,0:T(8,128)(2,1)} %param.14) | copy-start | bytes 2359300
  62.6 62.7 %copy-start.15 = (f32[1536]{0:T(1024)S(1)}, f32[1536]{0:T(1024)}, u32[]{:S(2)}) copy-start(f32[1536]{0:T(1024)} %param.19) | copy-start | bytes 18436
  63.4 114.4 %all-gather.8.cloned.1.call-start = ((), (), s32[]{:S(2)}) async-start(), calls=%async_computation.4 | async-start | bytes 5308416 | tf_op jit(solution)/shard_map/all_gather | solution.py:54
  165.7 8.3 %copy-start.18 = (f32[256,6,2048]{2,0,1:T(8,128)S(1)}, f32[256,6,2048]{2,0,1:T(8,128)}, u32[]{:S(2)}) copy-start(f32[256,6,2048]{2,0,1:T(8,128)} %get-tuple-element.7) | copy-start | bytes 37748740
  174.0 3.7 %copy-start.6 = (bf16[256,1536]{1,0:T(8,128)(2,1)S(1)}, bf16[256,1536]{1,0:T(8,128)(2,1)}, u32[]{:S(2)}) copy-start(bf16[256,1536]{1,0:T(8,128)(2,1)} %param.14) | copy-start | bytes 2359300
  177.7 5.1 %copy-start.13 = (f32[1536]{0:T(1024)S(1)}, f32[1536]{0:T(1024)}, u32[]{:S(2)}) copy-start(f32[1536]{0:T(1024)} %param.24) | copy-start | bytes 18436
  181.6 1.2 copy-start.3
  183.0 0.9 copy-start.1
  183.9 3.4 copy-start.12
  270.2 4.9 %copy-start.8 = (s32[256,4]{0,1:T(4,128)S(1)}, s32[256,4]{0,1:T(4,128)}, u32[]{:S(2)}) copy-start(s32[256,4]{0,1:T(4,128)} %param.18) | copy-start | bytes 12292
  270.2 5.2 %copy-start.17 = (s32[1,16]{1,0:T(1,128)S(1)}, s32[1,16]{1,0:T(1,128)}, u32[]{:S(2)}) copy-start(s32[1,16]{1,0:T(1,128)} %param.17) | copy-start | bytes 196
  270.2 5.5 %copy-start.2 = (bf16[256,1536]{1,0:T(8,128)(2,1)S(1)}, bf16[256,1536]{1,0:T(8,128)(2,1)}, u32[]{:S(2)}) copy-start(bf16[256,1536]{1,0:T(8,128)(2,1)} %copy-done.1) | copy-start | bytes 2359300
  270.2 59.4 %all-to-all-start.1 = ((bf16[16,2,48,1536]{3,2,1,0:T(8,128)(2,1)}), bf16[16,2,48,1536]{3,2,1,0:T(8,128)(2,1)}, u32[]{:S(2)}, u32[]{:S(2)}) async-start(bf16[16,2,48,1536]{3,2,1,0:T(8,128)(2,1)} %copy.87), calls=%async_computation.1 | async-start | bytes 9437184 | tf_op jit(solution)/shard_map/all_to_all | solution.py:154
  343.1 7.5 %copy-start.4 = (f32[256,1536]{1,0:T(8,128)S(1)}, f32[256,1536]{1,0:T(8,128)}, u32[]{:S(2)}) copy-start(f32[256,1536]{1,0:T(8,128)} %copy-done.3) | copy-start | bytes 4718596
Sparse Core Ops, SparseCore 0:
  9.7 46.5 all-gather.3
  63.5 25.8 all-gather.5
  91.0 33.7 all-gather.7
where the time goes:
time: 365 us; the launch traced here: 358 us
  blocking collectives  103 us (28%)
  waiting for transfers between devices  90.1 us (25%)
  other arithmetic  49.3 us (14%)
  matrix products  49 us (13%)
  local copies, waits for them, and re-layouts  47.6 us (13%)
  between operations  14.4 us (4%)
  starting transfers between devices  5.02 us (1%)
    all_to_all x1, blocking collectives, shards(): lax.all_to_all(outgoing, 'dp', split_axis=0, concat_axis=0, tiled=True)  54.8 us
    all_gather x1, waiting for transfers between devices, shards(): lax.all_gather(query_key_value_weight, 'mp', axis=1, tiled=True)  46.9 us
    all_to_all x1, waiting for transfers between devices, shards(): lax.all_to_all(produced, 'dp', split_axis=0, concat_axis=0, tiled=True)  41.7 us
    sub x2, other arithmetic, shards(): expd = jnp.exp(scores - row_max)  27.1 us
    all_gather x1, blocking collectives, shards(): lax.all_gather(adapter_down_weight, 'dp', axis=0, tiled=True)  25.1 us
    all_gather x1, blocking collectives, shards(): lax.all_gather(adapter_up_weight, 'dp', axis=0, tiled=True)  23.2 us
    dot_general x2, matrix products, shards(): jnp.einsum('tgs,sd->tgd', probs, v_head, preferred_element_type=jnp.float32)  10.7 us
    dot_general x2, matrix products, shards(): jnp.einsum('tgd,sd->tgs', q_head, k_head, preferred_element_type=jnp.floa...  10.2 us
  transfers between devices with their start and end apart: 4, of which 2 were waited for; matrix products, arithmetic and copies ran while one was open for 22% of the time, Pallas kernels for 0%

commit v1 on v0

--- a/solution.py
+++ b/solution.py
@@ -8,6 +8,22 @@
 CAP = 48
 eps = 1e-06
 neg_fill = -1e30
+
+
+def collect(x, axis, dim):
+    ways, here, turn = (lax.axis_size(axis), lax.axis_index(axis), x.shape[dim])
+    lengths = [n * ways if d == dim else n for d, n in enumerate(x.shape)]
+    full = lax.dynamic_update_slice_in_dim(jnp.zeros(lengths, x.dtype), x, here * turn, axis=dim)
+    going_up = going_down = x
+    for far in range(1, ways // 2 + 1):
+        going_up = lax.ppermute(going_up, axis, [(d, (d + 1) % ways) for d in range(ways)])
+        full = lax.dynamic_update_slice_in_dim(full, going_up, (here - far) % ways * turn, axis=dim)
+        if 2 * far < ways:
+            going_down = lax.ppermute(going_down, axis, [(d, (d - 1) % ways) for d in range(ways)])
+            full = lax.dynamic_update_slice_in_dim(
+                full, going_down, (here + far) % ways * turn, axis=dim
+            )
+    return full
 
 
 def rms_norm(values, gains):
@@ -39,7 +55,7 @@
     expert_down_weight,
 ):
     adapter_down_map, adapter_up_map = (
-        lax.all_gather(adapter_down_weight, "dp", axis=0, tiled=True),
+        collect(adapter_down_weight, "dp", 0),
         lax.all_gather(adapter_up_weight, "dp", axis=0, tiled=True),
     )
     tokens_per_shard = tokens.shape[0]

time: 365 us -> 391 us (1.071)
  the two profiles are of different devices: /device:TPU:6 before, /device:TPU:2 now
where the time goes in v1:
time: 391 us; the launch traced here: 383 us
  waiting for transfers between devices  108 us (28%)
  blocking collectives  71.9 us (18%)
  matrix products  49 us (13%)
  other arithmetic  48.8 us (12%)
  local copies, waits for them, and re-layouts  47.7 us (12%)
  starting transfers between devices  43 us (11%)
  between operations  14.7 us (4%)
    all_to_all x1, blocking collectives, shards(): lax.all_to_all(outgoing, 'dp', split_axis=0, concat_axis=0, tiled=True)  48.9 us
    all_gather x1, waiting for transfers between devices, shards(): lax.all_gather(query_key_value_weight, 'mp', axis=1, tiled=True)  47.5 us
    all_to_all x1, waiting for transfers between devices, shards(): lax.all_to_all(produced, 'dp', split_axis=0, concat_axis=0, tiled=True)  39.7 us
    ppermute x7, starting transfers between devices, collect(): lax.ppermute(going_down, axis, [(d, (d - 1) % ways) for d in range(ways)])  35.6 us
    sub x2, other arithmetic, shards(): expd = jnp.exp(scores - row_max)  26.6 us
    all_gather x1, blocking collectives, shards(): lax.all_gather(adapter_up_weight, 'dp', axis=0, tiled=True)  23 us
    ppermute x8, waiting for transfers between devices, collect(): lax.ppermute(going_up, axis, [(d, (d + 1) % ways) for d in range(ways)])  20.1 us
    dot_general x2, matrix products, shards(): jnp.einsum('tgs,sd->tgd', probs, v_head, preferred_element_type=jnp.float32)  10.7 us
  transfers between devices with their start and end apart: 19, of which 9 were waited for; matrix products, arithmetic and copies ran while one was open for 20% of the time, Pallas kernels for 0%

profile of v1, /device:TPU:2, one launch (start us, length us, event | category | flops | bytes accessed | tf_op | source)
XLA Modules:
  0.0 383.2 jit_solution(9433456072929827761)
XLA Ops:
  9.4 47.5 %all-gather.4.cloned.1.call-done = bf16[1536,2048]{1,0:T(8,128)(2,1)} async-done(((bf16[1536,256]{1,0:T(8,128)(2,1)}), bf16[1536,2048]{1,0:T(8,128)(2,1)}) %all-gather.4.cloned.1.call-update) | async-done | bytes 6291472 | tf_op jit(solution)/shard_map/all_gather | solution.py:69
  56.9 4.9 %fusion.49 = f32[256,2048]{1,0:T(8,128)S(1)} fusion(bf16[1536,2048]{1,0:T(8,128)(2,1)} %all-gather.4.cloned.1.call-done, bf16[256,1536]{1,0:T(8,128)(2,1)} %param.14, f32[1536]{0:T(1024)} %param.19, f32[256]{0:T(256)S(1)} %add_rsqrt_fusion.1), kind=kOutput, calls=%fused_computation.68 | convolution fusion | flops 1612185600 | bytes 9182208 | tf_op jit(solution)/shard_map/dot_general | solution.py:72
  65.5 3.9 %collective-permute-start.1 = (bf16[1,1536,16]{1,2,0:T(8,128)(2,1)S(1)}, bf16[1,1536,16]{1,2,0:T(8,128)(2,1)S(1)}, u32[]{:S(2)}, u32[]{:S(2)}) collective-permute-start(bf16[1,1536,16]{1,2,0:T(8,128)(2,1)S(1)} %copy-done.10), channel_id=1, source_target_pairs={{0,120},{8,0},{16,8},{24,16},{32,24},{40,32},{48,40},{56,48},{64,5... | collective-permute-start | bytes 147464 | tf_op jit(solution)/shard_map/ppermute | solution.py:22
  71.8 9.0 %reduce-window.19 = s32[32,8,128]{2,1,0:T(8,128)S(1)} reduce-window(s32[32,8,128]{2,1,0:T(8,128)S(1)} %fusion.54, s32[]{:T(128)} %constant.133.clone.1), window={size=1x1x128 pad=0_0x0_0x127_0}, to_apply=%region_9.10 | reduce-window | flops 4161536 | bytes 262148 | tf_op jit(solution)/shard_map/reduce-window.1
  82.3 23.0 %all_gather.13 = bf16[16,16,1536]{2,1,0:T(8,128)(2,1)S(1)} all-gather(bf16[1,16,1536]{2,1,0:T(8,128)(2,1)S(1)} %copy-done.9), channel_id=1, replica_groups=mesh['dp'=16,'mp'=8] {'dp'}, dimensions={0}, use_global_device_ids=true | all-gather | bytes 835584 | tf_op jit(solution)/shard_map/all_gather | solution.py:59
  105.9 5.0 %collective-permute-start.3 = (bf16[1,1536,16]{1,2,0:T(8,128)(2,1)S(1)}, bf16[1,1536,16]{1,2,0:T(8,128)(2,1)S(1)}, u32[]{:S(2)}, u32[]{:S(2)}) collective-permute-start(bf16[1,1536,16]{1,2,0:T(8,128)(2,1)S(1)} %collective-permute-done.1), channel_id=1, source_target_pairs={{0,120},{8,0},{16,8},{24,16},{32,24},{40,32},{48,40},{56,48},{64,5... | collective-permute-start | bytes 147464 | tf_op jit(solution)/shard_map/ppermute | solution.py:22
  113.4 5.3 %collective-permute-start.5 = (bf16[1,1536,16]{1,2,0:T(8,128)(2,1)S(1)}, bf16[1,1536,16]{1,2,0:T(8,128)(2,1)S(1)}, u32[]{:S(2)}, u32[]{:S(2)}) collective-permute-start(bf16[1,1536,16]{1,2,0:T(8,128)(2,1)S(1)} %collective-permute-done.3), channel_id=1, source_target_pairs={{0,120},{8,0},{16,8},{24,16},{32,24},{40,32},{48,40},{56,48},{64,5... | collective-permute-start | bytes 147464 | tf_op jit(solution)/shard_map/ppermute | solution.py:22
  120.8 5.3 %collective-permute-start.7 = (bf16[1,1536,16]{1,2,0:T(8,128)(2,1)S(1)}, bf16[1,1536,16]{1,2,0:T(8,128)(2,1)S(1)}, u32[]{:S(2)}, u32[]{:S(2)}) collective-permute-start(bf16[1,1536,16]{1,2,0:T(8,128)(2,1)S(1)} %collective-permute-done.5), channel_id=1, source_target_pairs={{0,120},{8,0},{16,8},{24,16},{32,24},{40,32},{48,40},{56,48},{64,5... | collective-permute-start | bytes 147464 | tf_op jit(solution)/shard_map/ppermute | solution.py:22
  128.3 5.3 %collective-permute-start.9 = (bf16[1,1536,16]{1,2,0:T(8,128)(2,1)S(1)}, bf16[1,1536,16]{1,2,0:T(8,128)(2,1)S(1)}, u32[]{:S(2)}, u32[]{:S(2)}) collective-permute-start(bf16[1,1536,16]{1,2,0:T(8,128)(2,1)S(1)} %collective-permute-done.7), channel_id=1, source_target_pairs={{0,120},{8,0},{16,8},{24,16},{32,24},{40,32},{48,40},{56,48},{64,5... | collective-permute-start | bytes 147464 | tf_op jit(solution)/shard_map/ppermute | solution.py:22
  135.7 5.3 %collective-permute-start.11 = (bf16[1,1536,16]{1,2,0:T(8,128)(2,1)S(1)}, bf16[1,1536,16]{1,2,0:T(8,128)(2,1)S(1)}, u32[]{:S(2)}, u32[]{:S(2)}) collective-permute-start(bf16[1,1536,16]{1,2,0:T(8,128)(2,1)S(1)} %collective-permute-done.9), channel_id=1, source_target_pairs={{0,120},{8,0},{16,8},{24,16},{32,24},{40,32},{48,40},{56,48},{64,5... | collective-permute-start | bytes 147464 | tf_op jit(solution)/shard_map/ppermute | solution.py:22
  143.1 5.3 %collective-permute-start.13 = (bf16[1,1536,16]{1,2,0:T(8,128)(2,1)S(1)}, bf16[1,1536,16]{1,2,0:T(8,128)(2,1)S(1)}, u32[]{:S(2)}, u32[]{:S(2)}) collective-permute-start(bf16[1,1536,16]{1,2,0:T(8,128)(2,1)S(1)} %collective-permute-done.11), channel_id=1, source_target_pairs={{0,120},{8,0},{16,8},{24,16},{32,24},{40,32},{48,40},{56,48},{64,5... | collective-permute-start | bytes 147464 | tf_op jit(solution)/shard_map/ppermute | solution.py:22
  151.0 7.3 %collective-permute-done.14 = bf16[1,1536,16]{1,2,0:T(8,128)(2,1)S(1)} collective-permute-done((bf16[1,1536,16]{1,2,0:T(8,128)(2,1)S(1)}, bf16[1,1536,16]{1,2,0:T(8,128)(2,1)S(1)}, u32[]{:S(2)}, u32[]{:S(2)}) %collective-permute-start.14) | collective-permute-done | bytes 49184 | tf_op jit(solution)/shard_map/ppermute | solution.py:19
  158.4 2.6 fusion.26
  161.4 7.3 %fusion.46 = f32[256,6,2048]{2,0,1:T(8,128)} fusion(bf16[256,6,128]{0,2,1:T(8,128)(2,1)S(1)} %bitcast.93, bf16[2048,512]{1,0:T(8,128)(2,1)} %all-gather.6.cloned.1.call-done), kind=kOutput, calls=%fused_computation.66 | convolution fusion | flops 805306368 | bytes 13500416 | tf_op jit(solution)/shard_map/tgd,sd->tgs/dot_general | solution.py:121
  168.8 2.9 fusion.45
  171.6 17.2 %fusion.70 = (f32[256,6]{0,1:T(8,128)S(1)}, f32[256,6,2048]{2,0,1:T(8,128)}) fusion(f32[256,6,2048]{2,0,1:T(8,128)} %fusion.46, pred[256,2048]{1,0:T(8,128)(4,1)} %fusion.31), kind=kOutput, calls=%fused_computation.128 | output fusion | flops 18876416 | bytes 25696256 | tf_op jit(solution)/shard_map/sub | solution.py:126
  188.8 9.5 %fusion.69 = (f32[256,6]{0,1:T(8,128)S(1)}, f32[256,6,2048]{2,0,1:T(8,128)}) fusion(f32[256,6,2048]{2,0,1:T(8,128)S(1)} %fusion.45, pred[256,2048]{1,0:T(8,128)(4,1)} %fusion.31), kind=kOutput, calls=%fused_computation.127 | output fusion | flops 18876416 | bytes 25696256 | tf_op jit(solution)/shard_map/sub | solution.py:126
  198.3 7.0 %fusion.36 = bf16[256,6,128]{0,2,1:T(8,128)(2,1)S(1)} fusion(f32[256,6,2048]{2,0,1:T(8,128)} %get-tuple-element.9, f32[256,6]{0,1:T(8,128)S(1)} %get-tuple-element.8, bf16[2048,512]{1,0:T(8,128)(2,1)} %all-gather.6.cloned.1.call-done), kind=kOutput, calls=%fused_computation.53 | convolution fusion | flops 811794432 | bytes 13506560 | tf_op jit(solution)/shard_map/tgs,sd->tgd/dot_general | solution.py:128
  206.6 3.7 fusion.35
  210.3 3.9 %multiply_reduce_fusion.1 = (f32[256]{0:T(256)S(1)}, f32[256,1536]{1,0:T(8,128)S(1)}) fusion(bf16[1536,1536]{0,1:T(8,128)(2,1)} %all-gather.8.cloned.1.call-done, bf16[256,768]{0,1:T(8,128)(2,1)S(1)} %bitcast.107, bf16[256,768]{0,1:T(8,128)(2,1)S(1)} %bitcast.106, bf16[256,1536]{1,0:T(8,128)(2,1)S(1)} %copy-done.6), kind=kOutput, calls=%fused_computation.51 | convolution fusion | flops 1211891456 | bytes 7865344 | tf_op jit(solution)/shard_map/dot_general | solution.py:131
  219.9 9.2 %scatter_custom_fusion = bf16[1536,1536]{1,0:T(8,128)(2,1)} fusion(s32[1024]{0:T(1024)S(1)} %bitcast.99, bf16[1024,1536]{1,0:T(8,128)(2,1)} %reshape.285, bf16[]{:T(256)} %constant.137.clone.1), kind=kCustom, calls=%fused_computation.42 | custom fusion | bytes 4719104 | tf_op jit(solution)/shard_map/scatter | solution.py:154
  229.1 48.9 %all_to_all.10 = bf16[16,2,48,1536]{3,2,1,0:T(8,128)(2,1)S(1)} all-to-all(bf16[16,2,48,1536]{3,2,1,0:T(8,128)(2,1)} %bitcast.92), channel_id=1, replica_groups=mesh['dp'=16,'mp'=8] {'dp'}, dimensions={0} | all-to-all | bytes 9437184 | tf_op jit(solution)/shard_map/all_to_all | solution.py:159
  278.0 10.0 %fusion.14 = f32[16,2,48,1536]{3,2,0,1:T(8,128)S(1)} fusion(bf16[2,1536,1536]{2,1,0:T(8,128)(2,1)} %param.26, bf16[16,2,48,1536]{3,2,1,0:T(8,128)(2,1)S(1)} %all_to_all.10), kind=kOutput, calls=%fused_computation.25 | convolution fusion | flops 7247757312 | bytes 23592960 | tf_op jit(solution)/shard_map/secd,edf->secf/dot_general | solution.py:160
  288.0 6.4 %convert_bitcast_fusion = bf16[16,2,48,1536]{3,2,0,1:T(8,128)(2,1)S(1)} fusion(bf16[2,768,1536]{2,1,0:T(8,128)(2,1)} %param.27, f32[16,2,48,1536]{3,2,0,1:T(8,128)S(1)} %fusion.14), kind=kOutput, calls=%fused_computation.32 | convolution fusion | flops 3629776896 | bytes 18874368 | tf_op jit(solution)/shard_map/secf,efd->secd/dot_general | solution.py:167
  294.3 2.6 copy.87
  296.9 4.9 %all-to-all-start.1 = ((bf16[16,2,48,1536]{3,2,1,0:T(8,128)(2,1)}), bf16[16,2,48,1536]{3,2,1,0:T(8,128)(2,1)}, u32[]{:S(2)}, u32[]{:S(2)}) async-start(bf16[16,2,48,1536]{3,2,1,0:T(8,128)(2,1)} %copy.87), calls=%async_computation.1 | async-start | bytes 9437184 | tf_op jit(solution)/shard_map/all_to_all | solution.py:170
  302.7 8.7 %gather_fusion.2 = f32[1024]{0:T(1024)S(1)} fusion(f32[256,32]{0,1:T(8,128)S(1)} %fusion.71, s32[1024]{0:T(1024)S(1)} %reshape.275), kind=kCustom, calls=%fused_computation.2 | custom fusion | bytes 16384 | tf_op jit(solution)/shard_map/jit(take_along_axis)/gather | solution.py:141
  311.8 2.9 gather_fusion.1
  314.7 39.7 %all-to-all-done.1 = bf16[16,2,48,1536]{3,2,1,0:T(8,128)(2,1)} async-done(((bf16[16,2,48,1536]{3,2,1,0:T(8,128)(2,1)}), bf16[16,2,48,1536]{3,2,1,0:T(8,128)(2,1)}, u32[]{:S(2)}, u32[]{:S(2)}) %all-to-all-start.1) | async-done | bytes 4718624 | tf_op jit(solution)/shard_map/all_to_all | solution.py:170
  354.4 9.6 %gather_fusion = bf16[1024,1536]{1,0:T(8,128)(2,1)S(1)} fusion(bf16[1536,1536]{1,0:T(8,128)(2,1)} %bitcast.28, s32[1024]{0:T(1024)S(1)} %broadcast_clamp_fusion), kind=kCustom, calls=%fused_computation | custom fusion | bytes 6295552 | tf_op jit(solution)/shard_map/gather | solution.py:172
  364.0 3.9 %reshape.258 = f32[256,4,1536]{2,1,0:T(4,128)} reshape(bf16[1024,1536]{1,0:T(8,128)(2,1)S(1)} %gather_fusion) | data formatting | bytes 9437184 | tf_op jit(solution)/shard_map/convert_element_type | solution.py:173
  367.9 7.5 %multiply_reduce_fusion = f32[256,1536]{1,0:T(8,128)S(1)} fusion(f32[256,4,1536]{2,1,0:T(4,128)} %reshape.258, f32[256,4]{1,0:T(8,128)S(1)} %copy.90), kind=kLoop, calls=%fused_computation.16 | loop fusion | flops 2752512 | bytes 7868416 | tf_op jit(solution)/shard_map/reduce_sum | solution.py:176
  (133 shorter events, 33.0 us)
Async XLA Ops:
  7.2 295.2 %copy-start = (bf16[1536,32]{0,1:T(8,128)(2,1)S(1)}, bf16[1536,32]{0,1:T(8,128)(2,1)}, u32[]{:S(2)}) copy-start(bf16[1536,32]{0,1:T(8,128)(2,1)} %param.25) | copy-start | bytes 294916
  7.2 49.7 %all-gather.4.cloned.1.call-start = ((), (), s32[]{:S(2)}) async-start(), calls=%async_computation.2 | async-start | bytes 7077888 | tf_op jit(solution)/shard_map/all_gather | solution.py:69
  7.9 153.5 %all-gather.6.cloned.1.call-start = ((), (), s32[]{:S(2)}) async-start(), calls=%async_computation.3 | async-start | bytes 2359296 | tf_op jit(solution)/shard_map/all_gather | solution.py:103
  9.3 54.6 %copy-start.10 = (bf16[1,1536,16]{1,2,0:T(8,128)(2,1)S(1)}, bf16[1,1536,16]{1,2,0:T(8,128)(2,1)}, u32[]{:S(2)}) copy-start(bf16[1,1536,16]{1,2,0:T(8,128)(2,1)} %param.21) | copy-start | bytes 147460
  9.3 60.1 %copy-start.7 = (s32[256,4]{0,1:T(4,128)S(1)}, s32[256,4]{0,1:T(4,128)}, u32[]{:S(2)}) copy-start(s32[256,4]{0,1:T(4,128)} %param.18) | copy-start | bytes 12292
  9.4 60.5 %copy-start.16 = (s32[1,4]{1,0:T(1,128)S(1)}, s32[1,4]{1,0:T(1,128)}, u32[]{:S(2)}) copy-start(s32[1,4]{1,0:T(1,128)} %param.15) | copy-start | bytes 52
  9.4 60.8 %copy-start.14 = (s32[1,4]{1,0:T(1,128)S(1)}, s32[1,4]{1,0:T(1,128)}, u32[]{:S(2)}) copy-start(s32[1,4]{1,0:T(1,128)} %param.16) | copy-start | bytes 52
  63.1 19.2 %copy-start.9 = (bf16[1,16,1536]{2,1,0:T(8,128)(2,1)S(1)}, bf16[1,16,1536]{2,1,0:T(8,128)(2,1)}, u32[]{:S(2)}) copy-start(bf16[1,16,1536]{2,1,0:T(8,128)(2,1)} %param.22) | copy-start | bytes 147460
  63.1 95.2 %copy-start.5 = (bf16[256,1536]{1,0:T(8,128)(2,1)S(1)}, bf16[256,1536]{1,0:T(8,128)(2,1)}, u32[]{:S(2)}) copy-start(bf16[256,1536]{1,0:T(8,128)(2,1)} %param.14) | copy-start | bytes 2359300
  63.2 95.2 %copy-start.15 = (f32[1536]{0:T(1024)S(1)}, f32[1536]{0:T(1024)}, u32[]{:S(2)}) copy-start(f32[1536]{0:T(1024)} %param.19) | copy-start | bytes 18436
  63.9 146.4 %all-gather.8.cloned.1.call-start = ((), (), s32[]{:S(2)}) async-start(), calls=%async_computation.4 | async-start | bytes 5308416 | tf_op jit(solution)/shard_map/all_gather | solution.py:70
  64.0 41.5 %collective-permute-start = (bf16[1,1536,16]{1,2,0:T(8,128)(2,1)S(1)}, bf16[1,1536,16]{1,2,0:T(8,128)(2,1)S(1)}, u32[]{:S(2)}, u32[]{:S(2)}) collective-permute-start(bf16[1,1536,16]{1,2,0:T(8,128)(2,1)S(1)} %copy-done.10), channel_id=1, source_target_pairs={{0,8},{8,16},{16,24},{24,32},{32,40},{40,48},{48,56},{56,64},{64,7... | collective-permute-start | bytes 147464 | tf_op jit(solution)/shard_map/ppermute | solution.py:19
  65.5 40.4 %collective-permute-start.1 = (bf16[1,1536,16]{1,2,0:T(8,128)(2,1)S(1)}, bf16[1,1536,16]{1,2,0:T(8,128)(2,1)S(1)}, u32[]{:S(2)}, u32[]{:S(2)}) collective-permute-start(bf16[1,1536,16]{1,2,0:T(8,128)(2,1)S(1)} %copy-done.10), channel_id=1, source_target_pairs={{0,120},{8,0},{16,8},{24,16},{32,24},{40,32},{48,40},{56,48},{64,5... | collective-permute-start | bytes 147464 | tf_op jit(solution)/shard_map/ppermute | solution.py:22
  105.5 7.9 %collective-permute-start.2 = (bf16[1,1536,16]{1,2,0:T(8,128)(2,1)S(1)}, bf16[1,1536,16]{1,2,0:T(8,128)(2,1)S(1)}, u32[]{:S(2)}, u32[]{:S(2)}) collective-permute-start(bf16[1,1536,16]{1,2,0:T(8,128)(2,1)S(1)} %collective-permute-done), channel_id=1, source_target_pairs={{0,8},{8,16},{16,24},{24,32},{32,40},{40,48},{48,56},{56,64},{64,7... | collective-permute-start | bytes 147464 | tf_op jit(solution)/shard_map/ppermute | solution.py:19
  105.9 7.5 %collective-permute-start.3 = (bf16[1,1536,16]{1,2,0:T(8,128)(2,1)S(1)}, bf16[1,1536,16]{1,2,0:T(8,128)(2,1)S(1)}, u32[]{:S(2)}, u32[]{:S(2)}) collective-permute-start(bf16[1,1536,16]{1,2,0:T(8,128)(2,1)S(1)} %collective-permute-done.1), channel_id=1, source_target_pairs={{0,120},{8,0},{16,8},{24,16},{32,24},{40,32},{48,40},{56,48},{64,5... | collective-permute-start | bytes 147464 | tf_op jit(solution)/shard_map/ppermute | solution.py:22
  113.4 7.4 %collective-permute-start.4 = (bf16[1,1536,16]{1,2,0:T(8,128)(2,1)S(1)}, bf16[1,1536,16]{1,2,0:T(8,128)(2,1)S(1)}, u32[]{:S(2)}, u32[]{:S(2)}) collective-permute-start(bf16[1,1536,16]{1,2,0:T(8,128)(2,1)S(1)} %collective-permute-done.2), channel_id=1, source_target_pairs={{0,8},{8,16},{16,24},{24,32},{32,40},{40,48},{48,56},{56,64},{64,7... | collective-permute-start | bytes 147464 | tf_op jit(solution)/shard_map/ppermute | solution.py:19
  113.4 7.4 %collective-permute-start.5 = (bf16[1,1536,16]{1,2,0:T(8,128)(2,1)S(1)}, bf16[1,1536,16]{1,2,0:T(8,128)(2,1)S(1)}, u32[]{:S(2)}, u32[]{:S(2)}) collective-permute-start(bf16[1,1536,16]{1,2,0:T(8,128)(2,1)S(1)} %collective-permute-done.3), channel_id=1, source_target_pairs={{0,120},{8,0},{16,8},{24,16},{32,24},{40,32},{48,40},{56,48},{64,5... | collective-permute-start | bytes 147464 | tf_op jit(solution)/shard_map/ppermute | solution.py:22
  120.8 7.4 %collective-permute-start.6 = (bf16[1,1536,16]{1,2,0:T(8,128)(2,1)S(1)}, bf16[1,1536,16]{1,2,0:T(8,128)(2,1)S(1)}, u32[]{:S(2)}, u32[]{:S(2)}) collective-permute-start(bf16[1,1536,16]{1,2,0:T(8,128)(2,1)S(1)} %collective-permute-done.4), channel_id=1, source_target_pairs={{0,8},{8,16},{16,24},{24,32},{32,40},{40,48},{48,56},{56,64},{64,7... | collective-permute-start | bytes 147464 | tf_op jit(solution)/shard_map/ppermute | solution.py:19
  120.8 7.4 %collective-permute-start.7 = (bf16[1,1536,16]{1,2,0:T(8,128)(2,1)S(1)}, bf16[1,1536,16]{1,2,0:T(8,128)(2,1)S(1)}, u32[]{:S(2)}, u32[]{:S(2)}) collective-permute-start(bf16[1,1536,16]{1,2,0:T(8,128)(2,1)S(1)} %collective-permute-done.5), channel_id=1, source_target_pairs={{0,120},{8,0},{16,8},{24,16},{32,24},{40,32},{48,40},{56,48},{64,5... | collective-permute-start | bytes 147464 | tf_op jit(solution)/shard_map/ppermute | solution.py:22
  128.3 7.4 %collective-permute-start.8 = (bf16[1,1536,16]{1,2,0:T(8,128)(2,1)S(1)}, bf16[1,1536,16]{1,2,0:T(8,128)(2,1)S(1)}, u32[]{:S(2)}, u32[]{:S(2)}) collective-permute-start(bf16[1,1536,16]{1,2,0:T(8,128)(2,1)S(1)} %collective-permute-done.6), channel_id=1, source_target_pairs={{0,8},{8,16},{16,24},{24,32},{32,40},{40,48},{48,56},{56,64},{64,7... | collective-permute-start | bytes 147464 | tf_op jit(solution)/shard_map/ppermute | solution.py:19
  128.3 7.4 %collective-permute-start.9 = (bf16[1,1536,16]{1,2,0:T(8,128)(2,1)S(1)}, bf16[1,1536,16]{1,2,0:T(8,128)(2,1)S(1)}, u32[]{:S(2)}, u32[]{:S(2)}) collective-permute-start(bf16[1,1536,16]{1,2,0:T(8,128)(2,1)S(1)} %collective-permute-done.7), channel_id=1, source_target_pairs={{0,120},{8,0},{16,8},{24,16},{32,24},{40,32},{48,40},{56,48},{64,5... | collective-permute-start | bytes 147464 | tf_op jit(solution)/shard_map/ppermute | solution.py:22
  135.7 7.4 %collective-permute-start.10 = (bf16[1,1536,16]{1,2,0:T(8,128)(2,1)S(1)}, bf16[1,1536,16]{1,2,0:T(8,128)(2,1)S(1)}, u32[]{:S(2)}, u32[]{:S(2)}) collective-permute-start(bf16[1,1536,16]{1,2,0:T(8,128)(2,1)S(1)} %collective-permute-done.8), channel_id=1, source_target_pairs={{0,8},{8,16},{16,24},{24,32},{32,40},{40,48},{48,56},{56,64},{64,7... | collective-permute-start | bytes 147464 | tf_op jit(solution)/shard_map/ppermute | solution.py:19
  135.7 7.4 %collective-permute-start.11 = (bf16[1,1536,16]{1,2,0:T(8,128)(2,1)S(1)}, bf16[1,1536,16]{1,2,0:T(8,128)(2,1)S(1)}, u32[]{:S(2)}, u32[]{:S(2)}) collective-permute-start(bf16[1,1536,16]{1,2,0:T(8,128)(2,1)S(1)} %collective-permute-done.9), channel_id=1, source_target_pairs={{0,120},{8,0},{16,8},{24,16},{32,24},{40,32},{48,40},{56,48},{64,5... | collective-permute-start | bytes 147464 | tf_op jit(solution)/shard_map/ppermute | solution.py:22
  143.1 7.4 %collective-permute-start.12 = (bf16[1,1536,16]{1,2,0:T(8,128)(2,1)S(1)}, bf16[1,1536,16]{1,2,0:T(8,128)(2,1)S(1)}, u32[]{:S(2)}, u32[]{:S(2)}) collective-permute-start(bf16[1,1536,16]{1,2,0:T(8,128)(2,1)S(1)} %collective-permute-done.10), channel_id=1, source_target_pairs={{0,8},{8,16},{16,24},{24,32},{32,40},{40,48},{48,56},{56,64},{64,7... | collective-permute-start | bytes 147464 | tf_op jit(solution)/shard_map/ppermute | solution.py:19
  143.1 7.9 %collective-permute-start.13 = (bf16[1,1536,16]{1,2,0:T(8,128)(2,1)S(1)}, bf16[1,1536,16]{1,2,0:T(8,128)(2,1)S(1)}, u32[]{:S(2)}, u32[]{:S(2)}) collective-permute-start(bf16[1,1536,16]{1,2,0:T(8,128)(2,1)S(1)} %collective-permute-done.11), channel_id=1, source_target_pairs={{0,120},{8,0},{16,8},{24,16},{32,24},{40,32},{48,40},{56,48},{64,5... | collective-permute-start | bytes 147464 | tf_op jit(solution)/shard_map/ppermute | solution.py:22
  150.5 7.9 %collective-permute-start.14 = (bf16[1,1536,16]{1,2,0:T(8,128)(2,1)S(1)}, bf16[1,1536,16]{1,2,0:T(8,128)(2,1)S(1)}, u32[]{:S(2)}, u32[]{:S(2)}) collective-permute-start(bf16[1,1536,16]{1,2,0:T(8,128)(2,1)S(1)} %collective-permute-done.12), channel_id=1, source_target_pairs={{0,8},{8,16},{16,24},{24,32},{32,40},{40,48},{48,56},{56,64},{64,7... | collective-permute-start | bytes 147464 | tf_op jit(solution)/shard_map/ppermute | solution.py:19
  198.3 8.3 %copy-start.18 = (f32[256,6,2048]{2,0,1:T(8,128)S(1)}, f32[256,6,2048]{2,0,1:T(8,128)}, u32[]{:S(2)}) copy-start(f32[256,6,2048]{2,0,1:T(8,128)} %get-tuple-element.7) | copy-start | bytes 37748740
  210.3 5.1 %copy-start.13 = (f32[1536]{0:T(1024)S(1)}, f32[1536]{0:T(1024)}, u32[]{:S(2)}) copy-start(f32[1536]{0:T(1024)} %param.24) | copy-start | bytes 18436
  296.9 5.2 %copy-start.17 = (s32[1,16]{1,0:T(1,128)S(1)}, s32[1,16]{1,0:T(1,128)}, u32[]{:S(2)}) copy-start(s32[1,16]{1,0:T(1,128)} %param.17) | copy-start | bytes 196
  296.9 5.5 %copy-start.2 = (bf16[256,1536]{1,0:T(8,128)(2,1)S(1)}, bf16[256,1536]{1,0:T(8,128)(2,1)}, u32[]{:S(2)}) copy-start(bf16[256,1536]{1,0:T(8,128)(2,1)} %copy-done.1) | copy-start | bytes 2359300
  296.9 57.5 %all-to-all-start.1 = ((bf16[16,2,48,1536]{3,2,1,0:T(8,128)(2,1)}), bf16[16,2,48,1536]{3,2,1,0:T(8,128)(2,1)}, u32[]{:S(2)}, u32[]{:S(2)}) async-start(bf16[16,2,48,1536]{3,2,1,0:T(8,128)(2,1)} %copy.87), calls=%async_computation.1 | async-start | bytes 9437184 | tf_op jit(solution)/shard_map/all_to_all | solution.py:170
  367.9 7.5 %copy-start.4 = (f32[256,1536]{1,0:T(8,128)S(1)}, f32[256,1536]{1,0:T(8,128)}, u32[]{:S(2)}) copy-start(f32[256,1536]{1,0:T(8,128)} %copy-done.3) | copy-start | bytes 4718596
  (6 other events, 15.5 us)
Sparse Core Ops, SparseCore 0:
  9.7 47.1 all-gather.3
  64.0 25.3 all-gather.5
  91.1 34.4 all-gather.7
